TPU v7x, 32 devices: a whole 2x2x4 slice. The times are simulated.
32 devices in a mesh: row: 4 (over y, x), col: 4 (over z), cores: 2 (over core).
Axes of the slice: x: 2, y: 2, z: 4, core: 2. Of those that a mesh axis runs over, the one named last changes fastest.
Arguments:
- multipoles: bfloat16 [315, 2048], P(None, ('col', 'row')), may hold values from -6 to 6
- operators: bfloat16 [40, 315, 315], P('cores'), may hold values from -0.0078125 to 0.0078125
- classes: int32 [2048, 2048], P('row', 'col'), may hold values from 0 to 39, as said below
- separated: int32 [4, 4], P('row', 'col'), may hold values 0 or 1
- owners: int32 [2048], P('row'), may hold values from 0 to 7, as said below
Outputs:
- owned: float32 [315, 4096], P(None, ('row', 'col', 'cores'))
Inputs may be any that keep to these rules, and one draw needn't show every extreme that they name: `owners`: in each block of 512 cells (cells b * 512 to b * 512 + 511) no owner holds more than 128 cells, and in every block one owner holds exactly 128. Cell t sits at (t % 8, (t // 8) % 4, t // 32) on a periodic grid of 8 x 4 x 2048 // 32 cells; classes[t, s] depends only on the wrapped offset between the positions of t and s.
All inputs are finite; a program needn't handle non-finite values. No bound on the sum of `separated` on one device may be relied on, other than what follows from the above.
Results may differ from a plain program's by a relative error of at most 0.0029.
Values may be sent and summed in bfloat16 or wider, within the bound.
A program may use at most 64 MiB of HBM per device.

v0:
```python
import jax
import jax.numpy as jnp
from jax import lax
from jax.sharding import PartitionSpec as P


def shards(multipoles, operators, classes, separated, owners):
    count = operators.shape[0]
    targets, sources = classes.shape
    base = lax.axis_index("cores") * count
    moved = jnp.einsum(
        "kqp,ps->kqs",
        operators,
        lax.all_gather(multipoles, "row", axis=1, tiled=True),
        preferred_element_type=jnp.float32,
    ).astype(jnp.bfloat16)
    spread = separated.shape[1]
    wide_mask = jnp.repeat(separated[0], sources // spread)
    labels = jnp.arange(count, dtype=jnp.int32) + base
    pick = (
        (classes[None, :, :] == labels[:, None, None]) & (wide_mask[None, None, :] == 1)
    ).astype(jnp.bfloat16)
    partial_value = jnp.einsum("kts,kqs->qt", pick, moved, preferred_element_type=jnp.float32)
    group = lax.axis_size(("col", "cores"))
    slots = 2 * targets // group
    member = lax.axis_index(("col", "cores"))
    hit = (owners[None, :] == jnp.arange(group, dtype=jnp.int32)[:, None]).astype(jnp.int32)
    before = jnp.cumsum(hit, axis=1) - hit
    rank = jnp.sum(before * hit, axis=0)
    slot_ids = jnp.arange(slots, dtype=jnp.int32)
    share = lax.psum_scatter(partial_value, ("col", "cores"), scatter_dimension=1, tiled=True)
    width = share.shape[1]
    share_owner = lax.dynamic_slice_in_dim(owners, member * width, width)
    outgoing = jnp.where(
        share_owner[None, None, :] == jnp.arange(group, dtype=jnp.int32)[:, None, None],
        share[None, :, :],
        0.0,
    )
    incoming = lax.all_to_all(outgoing, ("col", "cores"), split_axis=0, concat_axis=0, tiled=True)
    place = ((owners[None, :] == member) & (rank[None, :] == slot_ids[:, None])).astype(jnp.float32)
    owned = jnp.einsum(
        "spj,csj->pc", incoming, place.reshape(slots, group, width), precision=lax.Precision.HIGHEST
    )
    return owned


def solution(mesh):
    return jax.shard_map(
        shards,
        mesh=mesh,
        in_specs=(
            P(None, ("col", "row")),
            P("cores", None, None),
            P("row", "col"),
            P("row", "col"),
            P("row"),
        ),
        out_specs=P(None, ("row", "col", "cores")),
        check_vma=False,
    )
```

profile of v0, /device:TPU:0, one launch (start us, length us, event | category | flops | bytes accessed | tf_op | source)
XLA Modules:
  0.0 97.6 jit_solution(1368173200117882711)
XLA Ops:
  6.5 0.0 reduce-scatter.2.cloned.1.call-start
  6.5 11.0 %all_gather.3 = bf16[315,512]{1,0:T(8,128)(2,1)S(1)} all-gather(bf16[315,128]{1,0:T(8,128)(2,1)} %param.5), channel_id=1, replica_groups=mesh['row'=4,'col'=4,'cores'=2] {'row'}, dimensions={1}, use_global_device_ids=true | all-gather | bytes 403200 | tf_op jit(solution)/shard_map/all_gather | solution.py:14
  18.2 0.0 copy-start
  18.2 12.6 %fusion.6 = f32[315,512]{0,1:T(8,128)} fusion(s32[512,512]{1,0:T(8,128)} %param.7, s32[20]{0:T(128)S(1)} %iota_add_fusion, pred[]{:T(512)} %bitcast.1, bf16[20,315,315]{2,1,0:T(8,128)(2,1)} %param.6, bf16[315,512]{1,0:T(8,128)(2,1)S(1)} %all_gather.3), kind=kOutput, calls=%fused_computation.7 | convolution fusion | flops 5348853760 | bytes 5985337 | tf_op jit(solution)/shard_map/kts,kqs->qt/dot_general | solution.py:23
  30.8 0.0 reduce-scatter.2.cloned.1.call-update
  30.8 0.0 copy-done
  30.8 0.1 dynamic_slice.3
  30.9 31.8 %reduce-scatter.2.cloned.1.call-done = f32[315,64]{0,1:T(8,128)} async-done(((f32[315,512]{0,1:T(8,128)}), f32[315,64]{0,1:T(8,128)}) %reduce-scatter.2.cloned.1.call-update) | async-done | bytes 80656 | tf_op jit(solution)/shard_map/reduce_scatter | solution.py:31
  62.7 1.9 %broadcast_select_fusion = f32[8,315,64]{1,2,0:T(8,128)} fusion(f32[315,64]{0,1:T(8,128)} %reduce-scatter.2.cloned.1.call-done, pred[8,64]{1,0:T(8,128)(4,1)S(1)} %iota_compare_fusion.2), kind=kLoop, calls=%fused_computation.9 | loop fusion | flops 161280 | bytes 726272 | tf_op jit(solution)/shard_map/jit(_where)/select_n | solution.py:34
  64.7 3.5 %all-to-all-start = ((f32[8,315,64]{1,2,0:T(8,128)}), f32[8,315,64]{1,2,0:T(8,128)S(1)}, u32[]{:S(2)}, u32[]{:S(2)}) async-start(f32[8,315,64]{1,2,0:T(8,128)} %broadcast_select_fusion), calls=%async_computation.1 | async-start | bytes 1572864 | tf_op jit(solution)/shard_map/all_to_all | solution.py:39
  68.2 1.1 %reduce-window.6 = s32[8,4,128]{2,0,1:T(8,128)S(1)} reduce-window(s32[8,4,128]{2,0,1:T(8,128)S(1)} %fusion.15, s32[]{:T(128)} %constant.22.clone.1), window={size=1x1x128 pad=0_0x0_0x127_0}, to_apply=%region_1.2 | reduce-window | flops 520192 | bytes 32772 | tf_op jit(solution)/shard_map/reduce-window
  69.4 0.2 slice_reduce_fusion
  69.6 0.1 select_reduce_fusion
  69.7 0.1 eq.93
  69.8 0.1 and.23
  69.9 19.2 %all-to-all-done = f32[8,315,64]{1,2,0:T(8,128)S(1)} async-done(((f32[8,315,64]{1,2,0:T(8,128)}), f32[8,315,64]{1,2,0:T(8,128)S(1)}, u32[]{:S(2)}, u32[]{:S(2)}) %all-to-all-start) | async-done | bytes 645152 | tf_op jit(solution)/shard_map/all_to_all | solution.py:39
  89.1 1.6 %convolution_bitcast_fusion = f32[315,128]{1,0:T(8,128)} fusion(f32[8,315,64]{1,2,0:T(8,128)S(1)} %all-to-all-done, s32[8,64]{1,0:T(8,128)S(1)} %eq.93, pred[8,64]{1,0:T(8,128)(4,1)S(1)} %and.23), kind=kOutput, calls=%fused_computation.8 | convolution fusion | flops 247857152 | bytes 808960 | tf_op jit(solution)/shard_map/spj,csj->pc/dot_general | solution.py:41
  (6 shorter events, 0.1 us)
Async XLA Ops:
  6.5 56.2 %reduce-scatter.2.cloned.1.call-start = ((), (), s32[]{:S(2)}) async-start(), calls=%async_computation.2 | async-start | bytes 884736 | tf_op jit(solution)/shard_map/reduce_scatter | solution.py:31
  18.2 12.6 %copy-start = (s32[512]{0:T(512)S(1)}, s32[512]{0:T(512)}, u32[]{:S(2)}) copy-start(s32[512]{0:T(512)} %param.9) | copy-start | bytes 6148
  64.7 24.4 %all-to-all-start = ((f32[8,315,64]{1,2,0:T(8,128)}), f32[8,315,64]{1,2,0:T(8,128)S(1)}, u32[]{:S(2)}, u32[]{:S(2)}) async-start(f32[8,315,64]{1,2,0:T(8,128)} %broadcast_select_fusion), calls=%async_computation.1 | async-start | bytes 1572864 | tf_op jit(solution)/shard_map/all_to_all | solution.py:39
Sparse Core Ops, SparseCore 0:
  30.9 31.7 reduce-scatter.1
where the time goes:
time: 97.8 us; the launch traced here: 97.6 us
  waiting for transfers between devices  51.1 us (52%)
  matrix products  14.2 us (15%)
  between operations  14.1 us (14%)
  blocking collectives  11 us (11%)
  starting transfers between devices  3.55 us (4%)
  other arithmetic  3.2 us (3%)
    reduce_scatter x1, waiting for transfers between devices, shards(): lax.psum_scatter(partial_value, ('col', 'cores'), scatter_dimension=1, ti...  31.8 us
    all_to_all x1, waiting for transfers between devices, shards(): lax.all_to_all(outgoing, ('col', 'cores'), split_axis=0, concat_axis=0, t...  19.2 us
    dot_general x1, matrix products, shards(): jnp.einsum('kts,kqs->qt', pick, moved, preferred_element_type=jnp.float32)  12.6 us
    all_gather x1, blocking collectives, shards(): lax.all_gather(multipoles, 'row', axis=1, tiled=True)  11 us
    all_to_all x1, starting transfers between devices, shards(): lax.all_to_all(outgoing, ('col', 'cores'), split_axis=0, concat_axis=0, t...  3.55 us
  transfers between devices with their start and end apart: 2, of which 2 were waited for; matrix products, arithmetic and copies ran while one was open for 2% of the time, Pallas kernels for 0%

commit v1 on v0

v1 whole, which is shorter than its diff:
```python
import functools

import jax
import jax.numpy as jnp
from jax import lax
from jax.experimental import pallas as pl
from jax.experimental.pallas import tpu as pltpu
from jax.sharding import PartitionSpec as P

MESH = pl.DeviceIdType.MESH
F32 = jnp.float32
BF16 = jnp.bfloat16


def split_rows(rows):
    first = (rows // 2 + 15) // 16 * 16
    return ((0, first), (first, rows - first))


def kernel(
    dims,
    mult_hbm,
    op_hbm,
    cls_hbm,
    sep_ref,
    own_ref,
    out_ref,
    gath,
    mult,
    ops,
    cls,
    pick,
    moved,
    acc,
    place,
    psend0,
    psend1,
    precv0,
    precv1,
    zsend0,
    zsend1,
    zrecv0,
    zrecv1,
    local_sem,
    g_send,
    g_recv,
    p_send,
    p_recv,
    z_send,
    z_recv,
):
    n_row, n_col, n_core, spread = dims
    rows, width = mult_hbm.shape
    count = op_hbm.shape[0]
    targets, sources = cls_hbm.shape
    slots = zsend0.shape[2]
    group = n_col * n_core
    row = lax.axis_index("row")
    col = lax.axis_index("col")
    core = lax.axis_index("cores")
    parts = split_rows(rows)
    psend, precv = (psend0, psend1), (precv0, precv1)
    zsend, zrecv = (zsend0, zsend1), (zrecv0, zrecv1)

    barrier = pltpu.get_barrier_semaphore()
    for d in range(1, n_row):
        pl.semaphore_signal(
            barrier, inc=1, device_id={"row": lax.rem(row + d, n_row)}, device_id_type=MESH
        )
    for d in range(1, n_col):
        pl.semaphore_signal(
            barrier, inc=1, device_id={"col": lax.rem(col + d, n_col)}, device_id_type=MESH
        )
    pl.semaphore_signal(barrier, inc=1, device_id={"cores": 1 - core}, device_id_type=MESH)

    cls_copy = pltpu.make_async_copy(cls_hbm, cls, local_sem.at[0])
    cls_copy.start()
    own_copy = pltpu.make_async_copy(mult_hbm, gath.at[row], local_sem.at[1])
    own_copy.start()
    op_copy = pltpu.make_async_copy(op_hbm, ops, local_sem.at[2])
    op_copy.start()

    pl.semaphore_wait(barrier, n_row - 1 + n_col - 1 + 1)

    gathers = []
    for d in range(1, n_row):
        copy = pltpu.make_async_remote_copy(
            src_ref=mult_hbm,
            dst_ref=gath.at[row],
            send_sem=g_send.at[d - 1],
            recv_sem=g_recv.at[d - 1],
            device_id={"row": lax.rem(row + d, n_row)},
            device_id_type=MESH,
        )
        copy.start()
        gathers.append(copy)

    cls_copy.wait()
    per = sources // spread
    for j in range(spread):
        flag = sep_ref[0, j]
        block = cls[:, j * per : (j + 1) * per]
        wanted = (block - core * count) * flag + (flag - 1)
        turned = wanted.astype(F32).T
        for k in range(count):
            pick[pl.ds(k * sources + j * per, per), :] = jnp.where(
                turned == float(k), 1.0, 0.0
            ).astype(BF16)

    owners = own_ref[...]
    ids = lax.broadcasted_iota(jnp.int32, (group, targets), 0)
    hit = jnp.where(ids == owners, 1.0, 0.0)
    upper = jnp.where(
        lax.broadcasted_iota(jnp.int32, (targets, targets), 0)
        < lax.broadcasted_iota(jnp.int32, (targets, targets), 1),
        1.0,
        0.0,
    ).astype(BF16)
    before = jnp.dot(hit.astype(BF16), upper, preferred_element_type=F32)
    rank = jnp.sum(before * hit, axis=0, keepdims=True)
    slot = lax.broadcasted_iota(jnp.int32, (slots, targets), 0).astype(F32)
    for c in range(n_col):
        mine = jnp.where(owners == c * n_core + core, rank, -1.0)
        place[:, c * slots : (c + 1) * slots] = jnp.where(slot == mine, 1.0, 0.0).T.astype(BF16)

    own_copy.wait()
    for copy in gathers:
        copy.wait()
    if width % 128 == 0:
        for r in range(n_row):
            mult[:, r * width : (r + 1) * width] = gath[r]
    else:
        mult[...] = jnp.concatenate([gath[r] for r in range(n_row)], axis=1)
    op_copy.wait()

    def translate(part):
        start, size = parts[part]

        @pl.loop(0, count, unroll=4)
        def _(k):
            at = pl.multiple_of(k * sources, sources)
            moved[part * parts[0][1] : part * parts[0][1] + size, pl.ds(at, sources)] = jnp.dot(
                ops[k, start : start + size, :], mult[...], preferred_element_type=F32
            ).astype(BF16)

    def collect(part):
        start, size = parts[part]
        chunk = 4 if count % 4 == 0 else 1
        acc[0:size, :] = jnp.zeros((size, targets), F32)

        @pl.loop(0, count // chunk)
        def _(g):
            at = pl.multiple_of(g * chunk * sources, chunk * sources)
            acc[0:size, :] += jnp.dot(
                moved[part * parts[0][1] : part * parts[0][1] + size, pl.ds(at, chunk * sources)],
                pick[pl.ds(at, chunk * sources), :],
                preferred_element_type=F32,
            )

    def pair_start(part):
        size = parts[part][1]
        psend[part][...] = acc[0:size, :].astype(BF16)
        copy = pltpu.make_async_remote_copy(
            src_ref=psend[part],
            dst_ref=precv[part],
            send_sem=p_send.at[part],
            recv_sem=p_recv.at[part],
            device_id={"cores": 1 - core},
            device_id_type=MESH,
        )
        copy.start()
        return copy

    def spread_start(part, pair):
        size = parts[part][1]
        pair.wait()
        both = (psend[part][...].astype(F32) + precv[part][...].astype(F32)).astype(BF16)
        if slots % 128 == 0:
            placed = jnp.dot(both, place[...], preferred_element_type=F32).astype(BF16)
            for c in range(n_col):
                zsend[part][c] = placed[:, c * slots : (c + 1) * slots]
        else:
            for c in range(n_col):
                zsend[part][c] = jnp.dot(
                    both, place[:, c * slots : (c + 1) * slots], preferred_element_type=F32
                ).astype(BF16)
        copies = []
        for d in range(1, n_col):
            to = lax.rem(col + d, n_col)
            copy = pltpu.make_async_remote_copy(
                src_ref=zsend[part].at[to],
                dst_ref=zrecv[part].at[d - 1],
                send_sem=z_send.at[part, d - 1],
                recv_sem=z_recv.at[part, d - 1],
                device_id={"col": to},
                device_id_type=MESH,
            )
            copy.start()
            copies.append(copy)
        return copies

    def finish(part, copies):
        start, size = parts[part]
        for copy in copies:
            copy.wait()
        total = zsend[part][col].astype(F32)
        for d in range(1, n_col):
            total += zrecv[part][d - 1].astype(F32)
        out_ref[start : start + size, :] = total

    translate(0)
    collect(0)
    pair0 = pair_start(0)
    translate(1)
    sends0 = spread_start(0, pair0)
    collect(1)
    pair1 = pair_start(1)
    sends1 = spread_start(1, pair1)
    finish(0, sends0)
    finish(1, sends1)


def solution(mesh):
    n_row, n_col, n_core = mesh.shape["row"], mesh.shape["col"], mesh.shape["cores"]

    def shards(multipoles, operators, classes, separated, owners):
        rows, width = multipoles.shape
        count = operators.shape[0]
        targets, sources = classes.shape
        slots = 2 * targets // (n_col * n_core)
        sizes = [size for _, size in split_rows(rows)]
        top = sizes[0] * 2
        hbm = pl.BlockSpec(memory_space=pl.ANY)
        dma = pltpu.SemaphoreType.DMA
        return pl.pallas_call(
            functools.partial(kernel, (n_row, n_col, n_core, separated.shape[1])),
            out_shape=jax.ShapeDtypeStruct((rows, slots), F32),
            in_specs=[
                hbm,
                hbm,
                hbm,
                pl.BlockSpec(memory_space=pltpu.SMEM),
                pl.BlockSpec(memory_space=pltpu.VMEM),
            ],
            out_specs=pl.BlockSpec(memory_space=pltpu.VMEM),
            scratch_shapes=[
                pltpu.VMEM((n_row, rows, width), BF16),
                pltpu.VMEM((rows, sources), BF16),
                pltpu.VMEM((count, rows, rows), BF16),
                pltpu.VMEM((targets, sources), jnp.int32),
                pltpu.VMEM((count * sources, targets), BF16),
                pltpu.VMEM((top, count * sources), BF16),
                pltpu.VMEM((sizes[0], targets), F32),
                pltpu.VMEM((targets, n_col * slots), BF16),
            ]
            + [pltpu.VMEM((size, targets), BF16) for size in sizes]
            + [pltpu.VMEM((size, targets), BF16) for size in sizes]
            + [pltpu.VMEM((n_col, size, slots), BF16) for size in sizes]
            + [pltpu.VMEM((n_col - 1, size, slots), BF16) for size in sizes]
            + [
                dma((3,)),
                dma((n_row - 1,)),
                dma((n_row - 1,)),
                dma((2,)),
                dma((2,)),
                dma((2, n_col - 1)),
                dma((2, n_col - 1)),
            ],
            compiler_params=pltpu.CompilerParams(
                collective_id=0, has_side_effects=True, vmem_limit_bytes=60 * 1024 * 1024
            ),
        )(multipoles, operators, classes, separated, owners.reshape(1, targets))

    return jax.shard_map(
        shards,
        mesh=mesh,
        in_specs=(
            P(None, ("col", "row")),
            P("cores", None, None),
            P("row", "col"),
            P("row", "col"),
            P("row"),
        ),
        out_specs=P(None, ("row", "col", "cores")),
        check_vma=False,
    )
```

time: 97.8 us -> 31.3 us (0.32)
  waiting for transfers between devices: 51.1 us -> 0 us
  Pallas kernels: 0 us -> 28.8 us
  matrix products: 14.2 us -> 0 us
  between operations: 14.1 us -> 0.66 us
  blocking collectives: 11 us -> 0 us
  starting transfers between devices: 3.55 us -> 0 us
  other arithmetic: 3.2 us -> 0 us
  local copies, waits for them, and re-layouts: 0.47 us -> 1.59 us
    reduce_scatter x1 -> x0, waiting for transfers between devices: 31.8 us -> none  [shards(): lax.psum_scatter(partial_value, ('col', 'cores'), scatter_dimension=1, ti...]
    pallas_call x0 -> x1, Pallas kernels: none -> 28.8 us  [shards(): pl.pallas_call(functools.partial(kernel, (n_row, n_col, n_core, separated...]
    all_to_all x1 -> x0, waiting for transfers between devices: 19.2 us -> none  [shards(): lax.all_to_all(outgoing, ('col', 'cores'), split_axis=0, concat_axis=0, t...]
    dot_general x2 -> x0, matrix products: 14.2 us -> none  [the longest x1 12.6 us: shards(): jnp.einsum('kts,kqs->qt', pick, moved, preferred_element_type=jnp.float32)]
    all_gather x1 -> x0, blocking collectives: 11 us -> none  [shards(): lax.all_gather(multipoles, 'row', axis=1, tiled=True)]
    all_to_all x1 -> x0, starting transfers between devices: 3.55 us -> none  [shards(): lax.all_to_all(outgoing, ('col', 'cores'), split_axis=0, concat_axis=0, t...]
    select_n x1 -> x0, other arithmetic: 1.9 us -> none  [shards(): jnp.where(share_owner[None, None, :] == jnp.arange(group, dtype=jnp.int32...]
    unnamed x2 -> x1, local copies, waits for them, and re-layouts: 0.01 us -> 1.59 us
  transfers between devices with their start and end apart: 2 -> 0, of which waited for: 2 -> 0; matrix products, arithmetic and copies ran while one was open for 2% -> 0% of each run, Pallas kernels for 0% -> 0%
where the time goes in v1:
time: 31.3 us; the launch traced here: 31.1 us
  Pallas kernels  28.8 us (92%)
  local copies, waits for them, and re-layouts  1.59 us (5%)
  between operations  0.66 us (2%)
    pallas_call x1, Pallas kernels, shards(): pl.pallas_call(functools.partial(kernel, (n_row, n_col, n_core, separated...  28.8 us
    unnamed x1, local copies, waits for them, and re-layouts  1.59 us

profile of v1, /device:TPU:0, one launch (start us, length us, event | category | flops | bytes accessed | tf_op | source)
XLA Modules:
  0.0 31.1 jit_solution(14415881431684632629)
XLA Ops:
  0.7 28.8 %shard_map.55 = f32[315,128]{1,0:T(8,128)} custom-call(bf16[315,128]{1,0:T(8,128)(2,1)} %mult_hbm.1, bf16[20,315,315]{2,1,0:T(8,128)(2,1)} %op_hbm.1, s32[512,512]{1,0:T(8,128)} %cls_hbm.1, s32[1,1]{1,0:T(1,128)S(6)} %copy.7.sep_ref, s32[1,512]{1,0:T(1,128)} %bitcast.1), custom_call_target="tpu_custom_call" | custom-call | tf_op jit(solution)/shard_map/pallas_call | solution.py:235
  29.5 1.6 %copy.8 = f32[315,128]{1,0:T(8,128)} copy(f32[315,128]{1,0:T(8,128)} %shard_map.55) | data formatting | bytes 322560
